TPU v7x, 32 devices: a whole 2x2x4 slice. The times are simulated.
32 devices in a mesh: dp: 8 (over z, x), row: 2 (over core), col: 2 (over y).
Axes of the slice: x: 2, y: 2, z: 4, core: 2. Of those that a mesh axis runs over, the one named last changes fastest.
Arguments:
- tokens: bfloat16 [2, 8, 256, 2048], P(None, None, 'dp', ('row', 'col')), may hold values from -57 to 57
- lengths: int32 [2, 8], replicated, may hold values from 64 to 256, as said below
- deal_order: int32 [2, 8], replicated, may hold values from 0 to 7, each once within a row
- attention_gain: float32 [2048], P(('row', 'col')), may hold values from 0.25 to 1.75
- query_weight: bfloat16 [2048, 2048], P('row', 'col'), may hold values from -0.1875 to 0.1875
- key_weight: bfloat16 [2048, 2048], P('row', 'col'), may hold values from -0.1875 to 0.1875
- value_weight: bfloat16 [2048, 2048], P('row', 'col'), may hold values from -0.125 to 0.125
- output_weight: bfloat16 [2048, 2048], P('col', 'row'), may hold values from -0.25 to 0.25
- feed_gain: float32 [2048], P(('row', 'col')), may hold values from 0.25 to 1.75
- gate_weight: bfloat16 [2048, 8192], P('row', 'col'), may hold values from -0.125 to 0.125
- up_weight: bfloat16 [2048, 8192], P('row', 'col'), may hold values from -0.125 to 0.125
- down_weight: bfloat16 [8192, 2048], P('col', 'row'), may hold values from -0.09375 to 0.09375
- cotangent: bfloat16 [2, 8, 256, 2048], P(None, 'dp', None, ('row', 'col')), may hold values from -6 to 6
Outputs:
- layer_output: bfloat16 [2, 8, 256, 2048], P(None, None, 'dp', ('row', 'col'))
- tokens_grad: bfloat16 [2, 8, 256, 2048], P(None, None, 'dp', ('row', 'col'))
- attention_gain_grad: float32 [2048], P(('row', 'col', 'dp'))
- query_grad: float32 [2048, 2048], P(('row', 'dp'), 'col')
- key_grad: float32 [2048, 2048], P(('row', 'dp'), 'col')
- value_grad: float32 [2048, 2048], P(('row', 'dp'), 'col')
- output_grad: float32 [2048, 2048], P(('col', 'dp'), 'row')
- feed_gain_grad: float32 [2048], P(('row', 'col', 'dp'))
- gate_grad: float32 [2048, 8192], P(('row', 'dp'), 'col')
- up_grad: float32 [2048, 8192], P(('row', 'dp'), 'col')
- down_grad: float32 [8192, 2048], P(('col', 'dp'), 'row')
Inputs may be any that keep to these rules, and one draw needn't show every extreme that they name: `lengths`: in each micro-batch one sequence has exactly 256 tokens. `deal_order`: each row holds every number of 0 to 7 once.
All inputs are finite; a program needn't handle non-finite values.
Results may differ from a plain program's by a relative error of at most 0.023.
Values may be sent and summed in bfloat16 or wider, within the bound.
A program may use at most 256 MiB of HBM per device.

v0:
```python
import math
import jax
import jax.numpy as jnp
from jax import lax
from jax.sharding import PartitionSpec as P

D = 2048
HEADS = 32
HEAD_DIM = 64
SL = 256
MICRO = 2
EPSILON = 1e-05
ROPE_THETA = 130000.0
MASKED_SCORE = -1000000000.0


def rope_tables(slot_count, head_width):
    half_width = head_width // 2
    frequency = jnp.exp(
        jnp.arange(half_width, dtype=jnp.float32) * (-2.0 * math.log(ROPE_THETA) / head_width)
    )
    angles = jnp.arange(slot_count, dtype=jnp.float32)[:, None] * frequency[None, :]
    return (jnp.cos(angles)[:, None, :], jnp.sin(angles)[:, None, :])


def rotate(values, cosine_table, sine_table):
    half_width = values.shape[-1] // 2
    first_half = values[..., :half_width]
    second_half = values[..., half_width:]
    return jnp.concatenate(
        [
            first_half * cosine_table - second_half * sine_table,
            second_half * cosine_table + first_half * sine_table,
        ],
        axis=-1,
    )


def unrotate(grads, cosine_table, sine_table):
    half_width = grads.shape[-1] // 2
    first_half = grads[..., :half_width]
    second_half = grads[..., half_width:]
    return jnp.concatenate(
        [
            first_half * cosine_table + second_half * sine_table,
            second_half * cosine_table - first_half * sine_table,
        ],
        axis=-1,
    )


def masked_scores(queries, key_rows, length):
    positions = jnp.arange(SL, dtype=jnp.int32)
    allowed = (positions[None, :] <= positions[:, None]) & (positions[None, :] < length)
    scores = jnp.einsum(
        "qhd,khd->hqk", queries, key_rows, preferred_element_type=jnp.float32
    ) * HEAD_DIM ** (-0.5)
    return jnp.where(allowed[None], scores, MASKED_SCORE)


def attend_forward(queries, key_rows, values, length):
    scores = masked_scores(queries, key_rows, length)
    row_top = jnp.max(scores, axis=-1, keepdims=True)
    exp_scores = jnp.exp(scores - row_top)
    row_total = jnp.sum(exp_scores, axis=-1, keepdims=True)
    softmax_out = (exp_scores / row_total).astype(jnp.bfloat16)
    mixed_heads = jnp.einsum(
        "hqk,khd->qhd", softmax_out, values, preferred_element_type=jnp.float32
    )
    return (mixed_heads, row_top + jnp.log(row_total))


def attend_backward(queries, key_rows, values, length, log_total, mixed_grad):
    softmax_out = jnp.exp(masked_scores(queries, key_rows, length) - log_total)
    softmax_grad = jnp.einsum(
        "qhd,khd->hqk", mixed_grad, values, preferred_element_type=jnp.float32
    )
    values_grad = jnp.einsum(
        "hqk,qhd->khd",
        softmax_out.astype(jnp.bfloat16),
        mixed_grad,
        preferred_element_type=jnp.float32,
    )
    row_inner = jnp.sum(softmax_out * softmax_grad, axis=-1, keepdims=True)
    scores_grad = (softmax_out * (softmax_grad - row_inner)).astype(jnp.bfloat16)
    queries_grad = jnp.einsum(
        "hqk,khd->qhd", scores_grad, key_rows, preferred_element_type=jnp.float32
    ) * HEAD_DIM ** (-0.5)
    keys_grad = jnp.einsum(
        "hqk,qhd->khd", scores_grad, queries, preferred_element_type=jnp.float32
    ) * HEAD_DIM ** (-0.5)
    return (queries_grad, keys_grad, values_grad)


def column_gather(values):
    return lax.all_gather(values, "col", axis=1, tiled=True)


def row_scatter(stacked):
    return lax.psum_scatter(stacked, "row", scatter_dimension=2, tiled=True)


def row_gather(stacked):
    return lax.all_gather(stacked, "row", axis=2, tiled=True)


def column_scatter(partial_rows):
    return lax.psum_scatter(
        partial_rows.astype(jnp.bfloat16), "col", scatter_dimension=1, tiled=True
    ).astype(jnp.float32)


def feature_total(row_values):
    return lax.psum(row_values, ("row", "col"))


def norm_scale(values):
    return lax.rsqrt(feature_total(jnp.sum(values * values, axis=1)) / D + EPSILON)


def norm_backward(normed_grad, values, inverse_rms, gain_vector, upstream):
    gain_piece = jnp.sum(normed_grad * values * inverse_rms[:, None], axis=0)
    feature_dot = feature_total(jnp.sum(normed_grad * gain_vector * values, axis=1))
    result = (
        upstream
        + normed_grad * gain_vector * inverse_rms[:, None]
        - values * (inverse_rms**3 * feature_dot / D)[:, None]
    )
    return (result, gain_piece)


def per_device(
    tokens,
    lengths,
    deal_order,
    attention_gain,
    query_weight,
    key_weight,
    value_weight,
    output_weight,
    feed_gain,
    gate_weight,
    up_weight,
    down_weight,
    cotangent,
):
    head_shape = (SL, HEADS // (lax.axis_size("row") * lax.axis_size("col")), HEAD_DIM)
    dealt_rows = lax.all_to_all(
        jnp.take_along_axis(tokens, deal_order[:, :, None, None], axis=1),
        "dp",
        split_axis=1,
        concat_axis=2,
        tiled=True,
    )
    own_order = lax.dynamic_slice_in_dim(deal_order, lax.axis_index("dp"), 1, 1)
    own_lengths = jnp.take_along_axis(lengths, own_order, axis=1)[:, 0]
    cosine_table, sine_table = rope_tables(SL, HEAD_DIM)
    qkv_weights = jnp.stack((query_weight, key_weight, value_weight))
    pair_weights = jnp.stack((gate_weight, up_weight))
    qkv_grad_sum = jnp.zeros(qkv_weights.shape, jnp.float32)
    output_grad_sum = jnp.zeros(output_weight.shape, jnp.float32)
    pair_grad_sum = jnp.zeros(pair_weights.shape, jnp.float32)
    down_grad_sum = jnp.zeros(down_weight.shape, jnp.float32)
    attention_gain_sum = jnp.zeros(attention_gain.shape, jnp.float32)
    feed_gain_sum = jnp.zeros(feed_gain.shape, jnp.float32)
    row_positions = jnp.arange(SL, dtype=jnp.int32)
    output_blocks = []
    grad_blocks = []
    for micro_index in range(MICRO):
        length = own_lengths[micro_index]
        residual_in = dealt_rows[micro_index, 0].astype(jnp.float32)
        upstream = (
            cotangent[micro_index, 0].astype(jnp.float32)
            * (row_positions < length).astype(jnp.float32)[:, None]
        )
        inverse_first = norm_scale(residual_in)
        normed_first = (residual_in * inverse_first[:, None] * attention_gain).astype(jnp.bfloat16)
        normed_first_all = column_gather(normed_first)
        projected = row_scatter(
            jnp.einsum(
                "rd,kde->kre", normed_first_all, qkv_weights, preferred_element_type=jnp.float32
            )
        )
        queries = rotate(projected[0].reshape(head_shape), cosine_table, sine_table).astype(
            jnp.bfloat16
        )
        key_rows = rotate(projected[1].reshape(head_shape), cosine_table, sine_table).astype(
            jnp.bfloat16
        )
        values = projected[2].reshape(head_shape).astype(jnp.bfloat16)
        mixed_heads, log_total = attend_forward(queries, key_rows, values, length)
        mixed_all = row_gather(mixed_heads.reshape(1, SL, -1).astype(jnp.bfloat16))[0]
        middle = residual_in + column_scatter(
            jnp.dot(mixed_all, output_weight, preferred_element_type=jnp.float32)
        )
        inverse_second = norm_scale(middle)
        normed_second = (middle * inverse_second[:, None] * feed_gain).astype(jnp.bfloat16)
        normed_second_all = column_gather(normed_second)
        gate_up = row_scatter(
            jnp.einsum(
                "rd,kde->kre", normed_second_all, pair_weights, preferred_element_type=jnp.float32
            )
        )
        swish_gate = gate_up[0] / (1.0 + jnp.exp(-gate_up[0]))
        hidden = (swish_gate * gate_up[1]).astype(jnp.bfloat16)
        hidden_all = row_gather(hidden[None])[0]
        layer_rows = middle + column_scatter(
            jnp.dot(hidden_all, down_weight, preferred_element_type=jnp.float32)
        )
        output_blocks.append(layer_rows.astype(jnp.bfloat16))
        top_all = column_gather(upstream.astype(jnp.bfloat16))
        down_grad_sum = down_grad_sum + jnp.einsum(
            "rf,rd->fd", hidden_all, top_all, preferred_element_type=jnp.float32
        )
        hidden_grad = row_scatter(
            jnp.einsum("rd,fd->rf", top_all, down_weight, preferred_element_type=jnp.float32)[None]
        )[0]
        sigmoid_gate = 1.0 / (1.0 + jnp.exp(-gate_up[0]))
        gate_grad = (
            hidden_grad * gate_up[1] * sigmoid_gate * (1.0 + gate_up[0] * (1.0 - sigmoid_gate))
        )
        pair_grad_all = row_gather(
            jnp.stack((gate_grad, hidden_grad * swish_gate)).astype(jnp.bfloat16)
        )
        pair_grad_sum = pair_grad_sum + jnp.einsum(
            "rd,kre->kde", normed_second_all, pair_grad_all, preferred_element_type=jnp.float32
        )
        second_grad = column_scatter(
            jnp.einsum(
                "kre,kde->rd", pair_grad_all, pair_weights, preferred_element_type=jnp.float32
            )
        )
        middle_grad, gain_piece = norm_backward(
            second_grad, middle, inverse_second, feed_gain, upstream
        )
        feed_gain_sum = feed_gain_sum + gain_piece
        branch_all = column_gather(middle_grad.astype(jnp.bfloat16))
        output_grad_sum = output_grad_sum + jnp.einsum(
            "rh,rd->hd", mixed_all, branch_all, preferred_element_type=jnp.float32
        )
        mixed_grad = row_scatter(
            jnp.einsum("rd,hd->rh", branch_all, output_weight, preferred_element_type=jnp.float32)[
                None
            ]
        )[0]
        queries_grad, keys_grad, values_grad = attend_backward(
            queries,
            key_rows,
            values,
            length,
            log_total,
            mixed_grad.reshape(head_shape).astype(jnp.bfloat16),
        )
        turned_back = jnp.stack(
            (
                unrotate(queries_grad, cosine_table, sine_table),
                unrotate(keys_grad, cosine_table, sine_table),
                values_grad,
            )
        )
        three_all = row_gather(turned_back.reshape(3, SL, -1).astype(jnp.bfloat16))
        qkv_grad_sum = qkv_grad_sum + jnp.einsum(
            "rd,kre->kde", normed_first_all, three_all, preferred_element_type=jnp.float32
        )
        first_grad = column_scatter(
            jnp.einsum("kre,kde->rd", three_all, qkv_weights, preferred_element_type=jnp.float32)
        )
        input_grad, gain_piece = norm_backward(
            first_grad, residual_in, inverse_first, attention_gain, middle_grad
        )
        attention_gain_sum = attention_gain_sum + gain_piece
        grad_blocks.append(input_grad.astype(jnp.bfloat16))
    reduced = (
        lax.psum_scatter(
            attention_gain_sum.astype(jnp.bfloat16), "dp", scatter_dimension=0, tiled=True
        ).astype(jnp.float32),
        lax.psum_scatter(
            qkv_grad_sum[0].astype(jnp.bfloat16), "dp", scatter_dimension=0, tiled=True
        ).astype(jnp.float32),
        lax.psum_scatter(
            qkv_grad_sum[1].astype(jnp.bfloat16), "dp", scatter_dimension=0, tiled=True
        ).astype(jnp.float32),
        lax.psum_scatter(
            qkv_grad_sum[2].astype(jnp.bfloat16), "dp", scatter_dimension=0, tiled=True
        ).astype(jnp.float32),
        lax.psum_scatter(
            output_grad_sum.astype(jnp.bfloat16), "dp", scatter_dimension=0, tiled=True
        ).astype(jnp.float32),
        lax.psum_scatter(
            feed_gain_sum.astype(jnp.bfloat16), "dp", scatter_dimension=0, tiled=True
        ).astype(jnp.float32),
        lax.psum_scatter(
            pair_grad_sum[0].astype(jnp.bfloat16), "dp", scatter_dimension=0, tiled=True
        ).astype(jnp.float32),
        lax.psum_scatter(
            pair_grad_sum[1].astype(jnp.bfloat16), "dp", scatter_dimension=0, tiled=True
        ).astype(jnp.float32),
        lax.psum_scatter(
            down_grad_sum.astype(jnp.bfloat16), "dp", scatter_dimension=0, tiled=True
        ).astype(jnp.float32),
    )
    returned_out, returned_grad = (
        lax.all_to_all(
            jnp.stack(output_blocks)[:, None], "dp", split_axis=2, concat_axis=1, tiled=True
        ),
        lax.all_to_all(
            jnp.stack(grad_blocks)[:, None], "dp", split_axis=2, concat_axis=1, tiled=True
        ),
    )
    slot_of = jnp.argsort(deal_order, axis=1)[:, :, None, None]
    layer_output = jnp.take_along_axis(returned_out, slot_of, axis=1)
    tokens_grad = jnp.take_along_axis(returned_grad, slot_of, axis=1)
    return (
        layer_output,
        tokens_grad,
        reduced[0],
        reduced[1],
        reduced[2],
        reduced[3],
        reduced[4],
        reduced[5],
        reduced[6],
        reduced[7],
        reduced[8],
    )


def solution(mesh):
    in_specs = (
        P(None, None, "dp", ("row", "col")),
        P(),
        P(),
        P(("row", "col")),
        P("row", "col"),
        P("row", "col"),
        P("row", "col"),
        P("col", "row"),
        P(("row", "col")),
        P("row", "col"),
        P("row", "col"),
        P("col", "row"),
        P(None, "dp", None, ("row", "col")),
    )
    out_specs = (
        P(None, None, "dp", ("row", "col")),
        P(None, None, "dp", ("row", "col")),
        P(("row", "col", "dp")),
        P(("row", "dp"), "col"),
        P(("row", "dp"), "col"),
        P(("row", "dp"), "col"),
        P(("col", "dp"), "row"),
        P(("row", "col", "dp")),
        P(("row", "dp"), "col"),
        P(("row", "dp"), "col"),
        P(("col", "dp"), "row"),
    )
    return jax.shard_map(
        per_device, mesh=mesh, in_specs=in_specs, out_specs=out_specs, check_vma=False
    )
```

profile of v0, /device:TPU:0, one launch (start us, length us, event | category | flops | bytes accessed | tf_op | source)
XLA Modules:
  0.0 1240.4 jit_solution(1370745527233818062)
XLA Ops:
  102.4 10.7 all_gather.60
  121.8 12.0 copy.158
  133.8 12.3 copy.159
  167.8 10.3 convolution_bitcast_fusion
  186.7 9.7 convolution_bitcast_fusion.3
  205.2 11.7 convolution_bitcast_fusion.1
  224.1 10.2 reduce-scatter.38.cloned.1.call-done
  250.8 10.1 fusion.24
  267.1 10.1 fusion.23
  287.7 11.2 reduce-scatter.60.cloned.1.call-done
  298.9 17.5 %reduce-scatter.52.cloned.1.call-done = bf16[256,512]{1,0:T(8,128)(2,1)} async-done(((bf16[256,1024]{1,0:T(8,128)(2,1)}), bf16[256,512]{1,0:T(8,128)(2,1)}) %reduce-scatter.52.cloned.1.call-update) | async-done | bytes 262160 | tf_op jit(solution)/shard_map/reduce_scatter | solution.py:108
  468.3 11.7 add_convert_fusion.1
  481.0 15.7 %fusion.74 = f32[2,4096,1024]{2,1,0:T(8,128)} fusion(bf16[2,256,4096]{1,2,0:T(8,128)(2,1)} %all-gather.11.cloned.1.call-done, bf16[256,1024]{1,0:T(8,128)(2,1)S(1)} %copy-done.32), kind=kOutput, calls=%fused_computation.147 | convolution fusion | flops 4294967296 | bytes 38273024 | tf_op jit(solution)/shard_map/rd,kre->kde/dot_general | solution.py:225
  496.8 19.1 %fusion = bf16[2,1024,4096]{1,2,0:T(8,128)(2,1)} fusion(f32[2,4096,1024]{2,1,0:T(8,128)} %fusion.74, bf16[2,256,4096]{1,2,0:T(8,128)(2,1)S(1)} %copy-done.23, bf16[256,1024]{1,0:T(8,128)(2,1)S(1)} %copy-done.30), kind=kOutput, calls=%fused_computation.5 | convolution fusion | flops 4311744512 | bytes 55050240 | tf_op jit(solution)/shard_map/rd,kre->kde/dot_general | solution.py:225
  515.9 11.7 slice_bitcast_fusion
  527.7 11.3 copy.220
  539.0 11.6 copy.218
  572.2 21.8 %all-to-all-done.1 = bf16[2,1,256,512]{3,0,1,2:T(2,128)(2,1)S(1)} async-done(((bf16[2,1,256,512]{3,0,1,2:T(2,128)(2,1)}), bf16[2,1,256,512]{3,0,1,2:T(2,128)(2,1)S(1)}, u32[]{:S(2)}, u32[]{:S(2)}) %all-to-all-start.1) | async-done | bytes 524320 | tf_op jit(solution)/shard_map/all_to_all | solution.py:303
  601.1 22.1 %all-reduce.6 = (bf16[512]{0:T(512)(128)(2,1)S(1)}, bf16[512]{0:T(512)(128)(2,1)S(1)}) all-reduce(bf16[512]{0:T(512)(128)(2,1)S(1)} %add_convert_fusion.15, bf16[512]{0:T(512)(128)(2,1)S(1)} %add_convert_fusion.14), channel_id=18, replica_groups=mesh['dp'=8,'row'=2,'col'=2] {'dp'}, use_global_device_ids=true, to_apply=%region_41.43.clone | all-reduce | flops 1024 | bytes 4096
  635.0 68.9 %reduce-scatter.72.cloned.1.call-done = bf16[128,1024]{1,0:T(8,128)(2,1)} async-done(((bf16[1024,1024]{1,0:T(8,128)(2,1)}), bf16[128,1024]{1,0:T(8,128)(2,1)}) %reduce-scatter.72.cloned.1.call-update) | async-done | bytes 262160
  705.9 68.8 %reduce-scatter.70.cloned.1.call-done = bf16[128,1024]{1,0:T(8,128)(2,1)} async-done(((bf16[1024,1024]{1,0:T(8,128)(2,1)}), bf16[128,1024]{1,0:T(8,128)(2,1)}) %reduce-scatter.70.cloned.1.call-update) | async-done | bytes 262160
  776.7 149.5 %reduce-scatter.68.cloned.1.call-done = bf16[512,1024]{1,0:T(8,128)(2,1)} async-done(((bf16[4096,1024]{1,0:T(8,128)(2,1)}), bf16[512,1024]{1,0:T(8,128)(2,1)}) %reduce-scatter.68.cloned.1.call-update) | async-done | bytes 1048592 | tf_op jit(solution)/shard_map/reduce_scatter | solution.py:298
  929.0 149.4 %reduce-scatter.78.cloned.1.call-done = bf16[128,4096]{1,0:T(8,128)(2,1)} async-done(((bf16[1024,4096]{1,0:T(8,128)(2,1)}), bf16[128,4096]{1,0:T(8,128)(2,1)}) %reduce-scatter.78.cloned.1.call-update) | async-done | bytes 1048592
  1081.6 148.4 %reduce-scatter.76.cloned.1.call-done = bf16[128,4096]{1,0:T(8,128)(2,1)} async-done(((bf16[1024,4096]{1,0:T(8,128)(2,1)}), bf16[128,4096]{1,0:T(8,128)(2,1)}) %reduce-scatter.76.cloned.1.call-update) | async-done | bytes 1048592
  (410 shorter events, 388.3 us)
Async XLA Ops:
  18.6 62.7 %reduce-scatter.42.cloned.1.call-start = ((), (), s32[]{:S(2)}) async-start(), calls=%async_computation.31 | async-start | bytes 4718592 | tf_op jit(solution)/shard_map/reduce_scatter | solution.py:100
  73.9 72.2 %reduce-scatter.36.cloned.1.call-start = ((), (), s32[]{:S(2)}) async-start(), calls=%async_computation.27 | async-start | bytes 786432 | tf_op jit(solution)/shard_map/reduce_scatter | solution.py:108
  92.7 53.4 %reduce-scatter.44.cloned.1.call-start = ((), (), s32[]{:S(2)}) async-start(), calls=%async_computation.32 | async-start | bytes 786432 | tf_op jit(solution)/shard_map/reduce_scatter | solution.py:108
  101.1 116.4 %reduce-scatter.58.cloned.1.call-start = ((), (), s32[]{:S(2)}) async-start(), calls=%async_computation.42 | async-start | bytes 6291456 | tf_op jit(solution)/shard_map/reduce_scatter | solution.py:100
  121.8 95.7 %reduce-scatter.46.cloned.1.call-start = ((), (), s32[]{:S(2)}) async-start(), calls=%async_computation.33 | async-start | bytes 12582912 | tf_op jit(solution)/shard_map/reduce_scatter | solution.py:100
  178.1 46.0 %reduce-scatter.50.cloned.1.call-start = ((), (), s32[]{:S(2)}) async-start(), calls=%async_computation.36 | async-start | bytes 6291456 | tf_op jit(solution)/shard_map/reduce_scatter | solution.py:100
  196.5 37.8 %reduce-scatter.38.cloned.1.call-start = ((), (), s32[]{:S(2)}) async-start(), calls=%async_computation.28 | async-start | bytes 12582912 | tf_op jit(solution)/shard_map/reduce_scatter | solution.py:100
  224.0 43.1 %all-gather.11.cloned.1.call-start = ((), (), s32[]{:S(2)}) async-start(), calls=%async_computation.37 | async-start | bytes 6291456 | tf_op jit(solution)/shard_map/all_gather | solution.py:104
  240.8 39.6 %all-gather.9.cloned.1.call-start = ((), (), s32[]{:S(2)}) async-start(), calls=%async_computation.34 | async-start | bytes 3145728 | tf_op jit(solution)/shard_map/all_gather | solution.py:104
  241.5 57.3 %reduce-scatter.60.cloned.1.call-start = ((), (), s32[]{:S(2)}) async-start(), calls=%async_computation.44 | async-start | bytes 786432 | tf_op jit(solution)/shard_map/reduce_scatter | solution.py:108
  261.0 55.4 %reduce-scatter.52.cloned.1.call-start = ((), (), s32[]{:S(2)}) async-start(), calls=%async_computation.38 | async-start | bytes 786432 | tf_op jit(solution)/shard_map/reduce_scatter | solution.py:108
  277.2 56.3 %reduce-scatter.48.cloned.1.call-start = ((), (), s32[]{:S(2)}) async-start(), calls=%async_computation.35 | async-start | bytes 786432 | tf_op jit(solution)/shard_map/reduce_scatter | solution.py:108
  287.6 72.9 %reduce-scatter.54.cloned.1.call-start = ((), (), s32[]{:S(2)}) async-start(), calls=%async_computation.39 | async-start | bytes 1572864 | tf_op jit(solution)/shard_map/reduce_scatter | solution.py:100
  358.1 45.5 %all-gather.13.cloned.1.call-start = ((), (), s32[]{:S(2)}) async-start(), calls=%async_computation.40 | async-start | bytes 2359296 | tf_op jit(solution)/shard_map/all_gather | solution.py:104
  403.6 147.2 %reduce-scatter.56.cloned.1.call-start = ((), (), s32[]{:S(2)}) async-start(), calls=%async_computation.41 | async-start | bytes 786432 | tf_op jit(solution)/shard_map/reduce_scatter | solution.py:108
  408.9 141.8 %reduce-scatter.64.cloned.1.call-start = ((), (), s32[]{:S(2)}) async-start(), calls=%async_computation.47 | async-start | bytes 786432 | tf_op jit(solution)/shard_map/reduce_scatter | solution.py:108
  419.1 141.5 %reduce-scatter.40.cloned.1.call-start = ((), (), s32[]{:S(2)}) async-start(), calls=%async_computation.30 | async-start | bytes 786432 | tf_op jit(solution)/shard_map/reduce_scatter | solution.py:108
  434.4 164.9 %reduce-scatter.66.cloned.1.call-start = ((), (), s32[]{:S(2)}) async-start(), calls=%async_computation.48 | async-start | bytes 2359296 | tf_op jit(solution)/shard_map/reduce_scatter | solution.py:286
  437.7 195.2 %reduce-scatter.74.cloned.1.call-start = ((), (), s32[]{:S(2)}) async-start(), calls=%async_computation.52 | async-start | bytes 2359296
  450.7 253.1 %reduce-scatter.72.cloned.1.call-start = ((), (), s32[]{:S(2)}) async-start(), calls=%async_computation.51 | async-start | bytes 2359296
  454.7 319.9 %reduce-scatter.70.cloned.1.call-start = ((), (), s32[]{:S(2)}) async-start(), calls=%async_computation.50 | async-start | bytes 2359296
  457.4 468.8 %reduce-scatter.68.cloned.1.call-start = ((), (), s32[]{:S(2)}) async-start(), calls=%async_computation.49 | async-start | bytes 9437184 | tf_op jit(solution)/shard_map/reduce_scatter | solution.py:298
  480.0 598.4 %reduce-scatter.78.cloned.1.call-start = ((), (), s32[]{:S(2)}) async-start(), calls=%async_computation.54 | async-start | bytes 9437184
  539.0 691.1 %reduce-scatter.76.cloned.1.call-start = ((), (), s32[]{:S(2)}) async-start(), calls=%async_computation.53 | async-start | bytes 9437184
  (94 other events, 825.1 us)
Sparse Core Ops, SparseCore 0:
  92.8 16.9 reduce-scatter.35
  112.6 14.3 reduce-scatter.43
  129.1 12.0 reduce-scatter.57
  178.2 17.2 reduce-scatter.45
  197.9 13.2 reduce-scatter.49
  217.1 17.1 reduce-scatter.37
  235.8 14.9 all-gather.14
  252.2 14.8 all-gather.10
  268.6 11.7 all-gather.8
  283.1 15.7 reduce-scatter.59
  301.8 14.5 reduce-scatter.51
  319.0 14.5 reduce-scatter.47
  402.9 10.8 all-gather.16
  415.4 11.7 all-gather.6
  429.9 15.7 reduce-scatter.55
  448.5 14.5 reduce-scatter.63
  466.0 14.5 reduce-scatter.39
  484.1 67.7 reduce-scatter.65
  555.3 77.5 reduce-scatter.73
  637.0 66.7 reduce-scatter.71
  707.8 66.8 reduce-scatter.69
  778.2 148.0 reduce-scatter.67
  930.3 148.0 reduce-scatter.77
  1082.0 147.9 reduce-scatter.75
  (5 shorter events, 46.1 us)
where the time goes:
time: 1250 us; the launch traced here: 1240 us
  waiting for transfers between devices  693 us (55%)
  matrix products  182 us (15%)
  local copies, waits for them, and re-layouts  140 us (11%)
  blocking collectives  125 us (10%)
  other arithmetic  65.1 us (5%)
  starting transfers between devices  19.2 us (2%)
  between operations  16.4 us (1%)
    unnamed x34, waiting for transfers between devices  443 us
    reduce_scatter x1, waiting for transfers between devices, per_device(): lax.psum_scatter(down_grad_sum.astype(jnp.bfloat16), 'dp', scatter_dimens...  149 us
    unnamed x195, local copies, waits for them, and re-layouts  97.5 us
    all_gather x8, blocking collectives, column_gather(): return lax.all_gather(values, 'col', axis=1, tiled=True)  69 us
    dot_general x2, matrix products, per_device(): jnp.einsum('rd,kre->kde', normed_second_all, pair_grad_all, preferred_ele...  34.9 us
    reduce_scatter x8, waiting for transfers between devices, column_scatter(): lax.psum_scatter(partial_rows.astype(jnp.bfloat16), 'col', scatter_dimens...  34.2 us
    all_gather x6, waiting for transfers between devices, row_gather(): return lax.all_gather(stacked, 'row', axis=2, tiled=True)  31.3 us
    psum x4, blocking collectives, feature_total(): return lax.psum(row_values, ('row', 'col'))  29.1 us
  transfers between devices with their start and end apart: 32, of which 17 were waited for; matrix products, arithmetic and copies ran while one was open for 26% of the time, Pallas kernels for 0%

commit v1 on v0

--- a/solution.py
+++ b/solution.py
@@ -111,7 +111,7 @@
 
 
 def feature_total(row_values):
-    return lax.psum(row_values, ("row", "col"))
+    return lax.psum(lax.psum(row_values, "col"), "row")
 
 
 def norm_scale(values):

time: 1250 us -> 1250 us (level)
    psum x4 -> x8, blocking collectives: 29.1 us -> 32.2 us  [feature_total(): return lax.psum(lax.psum(row_values, 'col'), 'row')]
  transfers between devices with their start and end apart: 32 -> 32, of which waited for: 17 -> 18; matrix products, arithmetic and copies ran while one was open for 26% -> 26% of each run, Pallas kernels for 0% -> 0%
where the time goes in v1:
time: 1250 us; the launch traced here: 1240 us
  waiting for transfers between devices  691 us (55%)
  matrix products  182 us (15%)
  local copies, waits for them, and re-layouts  140 us (11%)
  blocking collectives  128 us (10%)
  other arithmetic  65.1 us (5%)
  starting transfers between devices  19.5 us (2%)
  between operations  16.3 us (1%)
    unnamed x34, waiting for transfers between devices  443 us
    reduce_scatter x1, waiting for transfers between devices, per_device(): lax.psum_scatter(down_grad_sum.astype(jnp.bfloat16), 'dp', scatter_dimens...  149 us
    unnamed x195, local copies, waits for them, and re-layouts  97.8 us
    all_gather x8, blocking collectives, column_gather(): return lax.all_gather(values, 'col', axis=1, tiled=True)  69.4 us
    dot_general x2, matrix products, per_device(): jnp.einsum('rd,kre->kde', normed_second_all, pair_grad_all, preferred_ele...  34.9 us
    reduce_scatter x8, waiting for transfers between devices, column_scatter(): lax.psum_scatter(partial_rows.astype(jnp.bfloat16), 'col', scatter_dimens...  32.5 us
    psum x8, blocking collectives, feature_total(): return lax.psum(lax.psum(row_values, 'col'), 'row')  32.2 us
    all_gather x6, waiting for transfers between devices, row_gather(): return lax.all_gather(stacked, 'row', axis=2, tiled=True)  31.2 us
  transfers between devices with their start and end apart: 32, of which 18 were waited for; matrix products, arithmetic and copies ran while one was open for 26% of the time, Pallas kernels for 0%

profile of v1, /device:TPU:0, one launch (start us, length us, event | category | flops | bytes accessed | tf_op | source)
XLA Modules:
  0.0 1242.6 jit_solution(2050697084924025736)
XLA Ops:
  102.8 10.8 all_gather.60
  122.2 12.0 copy.158
  134.2 12.3 copy.159
  170.2 10.2 convolution_bitcast_fusion
  189.5 9.6 convolution_bitcast_fusion.3
  208.1 11.6 convolution_bitcast_fusion.1
  226.8 9.8 reduce-scatter.38.cloned.1.call-done
  253.1 10.1 fusion.24
  269.4 10.1 fusion.23
  289.9 11.2 reduce-scatter.60.cloned.1.call-done
  301.1 17.5 %reduce-scatter.52.cloned.1.call-done = bf16[256,512]{1,0:T(8,128)(2,1)} async-done(((bf16[256,1024]{1,0:T(8,128)(2,1)}), bf16[256,512]{1,0:T(8,128)(2,1)}) %reduce-scatter.52.cloned.1.call-update) | async-done | bytes 262160 | tf_op jit(solution)/shard_map/reduce_scatter | solution.py:108
  470.5 11.7 add_convert_fusion.1
  483.2 15.7 %fusion.74 = f32[2,4096,1024]{2,1,0:T(8,128)} fusion(bf16[2,256,4096]{1,2,0:T(8,128)(2,1)} %all-gather.11.cloned.1.call-done, bf16[256,1024]{1,0:T(8,128)(2,1)S(1)} %copy-done.32), kind=kOutput, calls=%fused_computation.147 | convolution fusion | flops 4294967296 | bytes 38273024 | tf_op jit(solution)/shard_map/rd,kre->kde/dot_general | solution.py:225
  499.0 19.1 %fusion = bf16[2,1024,4096]{1,2,0:T(8,128)(2,1)} fusion(f32[2,4096,1024]{2,1,0:T(8,128)} %fusion.74, bf16[2,256,4096]{1,2,0:T(8,128)(2,1)S(1)} %copy-done.23, bf16[256,1024]{1,0:T(8,128)(2,1)S(1)} %copy-done.30), kind=kOutput, calls=%fused_computation.5 | convolution fusion | flops 4311744512 | bytes 55050240 | tf_op jit(solution)/shard_map/rd,kre->kde/dot_general | solution.py:225
  518.1 11.8 slice_bitcast_fusion
  529.9 11.3 copy.220
  541.3 11.8 copy.218
  574.5 21.7 %all-to-all-done.1 = bf16[2,1,256,512]{3,0,1,2:T(2,128)(2,1)S(1)} async-done(((bf16[2,1,256,512]{3,0,1,2:T(2,128)(2,1)}), bf16[2,1,256,512]{3,0,1,2:T(2,128)(2,1)S(1)}, u32[]{:S(2)}, u32[]{:S(2)}) %all-to-all-start.1) | async-done | bytes 524320 | tf_op jit(solution)/shard_map/all_to_all | solution.py:303
  603.4 22.1 %all-reduce.10 = (bf16[512]{0:T(512)(128)(2,1)S(1)}, bf16[512]{0:T(512)(128)(2,1)S(1)}) all-reduce(bf16[512]{0:T(512)(128)(2,1)S(1)} %add_convert_fusion.15, bf16[512]{0:T(512)(128)(2,1)S(1)} %add_convert_fusion.14), channel_id=18, replica_groups=mesh['dp'=8,'row'=2,'col'=2] {'dp'}, use_global_device_ids=true, to_apply=%region_49.51.clone | all-reduce | flops 1024 | bytes 4096
  637.4 68.8 %reduce-scatter.72.cloned.1.call-done = bf16[128,1024]{1,0:T(8,128)(2,1)} async-done(((bf16[1024,1024]{1,0:T(8,128)(2,1)}), bf16[128,1024]{1,0:T(8,128)(2,1)}) %reduce-scatter.72.cloned.1.call-update) | async-done | bytes 262160
  708.2 68.8 %reduce-scatter.70.cloned.1.call-done = bf16[128,1024]{1,0:T(8,128)(2,1)} async-done(((bf16[1024,1024]{1,0:T(8,128)(2,1)}), bf16[128,1024]{1,0:T(8,128)(2,1)}) %reduce-scatter.70.cloned.1.call-update) | async-done | bytes 262160
  779.0 149.4 %reduce-scatter.68.cloned.1.call-done = bf16[512,1024]{1,0:T(8,128)(2,1)} async-done(((bf16[4096,1024]{1,0:T(8,128)(2,1)}), bf16[512,1024]{1,0:T(8,128)(2,1)}) %reduce-scatter.68.cloned.1.call-update) | async-done | bytes 1048592 | tf_op jit(solution)/shard_map/reduce_scatter | solution.py:298
  931.3 149.3 %reduce-scatter.78.cloned.1.call-done = bf16[128,4096]{1,0:T(8,128)(2,1)} async-done(((bf16[1024,4096]{1,0:T(8,128)(2,1)}), bf16[128,4096]{1,0:T(8,128)(2,1)}) %reduce-scatter.78.cloned.1.call-update) | async-done | bytes 1048592
  1083.8 148.4 %reduce-scatter.76.cloned.1.call-done = bf16[128,4096]{1,0:T(8,128)(2,1)} async-done(((bf16[1024,4096]{1,0:T(8,128)(2,1)}), bf16[128,4096]{1,0:T(8,128)(2,1)}) %reduce-scatter.76.cloned.1.call-update) | async-done | bytes 1048592
  (414 shorter events, 391.1 us)
Async XLA Ops:
  18.6 62.2 %reduce-scatter.42.cloned.1.call-start = ((), (), s32[]{:S(2)}) async-start(), calls=%async_computation.31 | async-start | bytes 4718592 | tf_op jit(solution)/shard_map/reduce_scatter | solution.py:100
  73.4 73.1 %reduce-scatter.36.cloned.1.call-start = ((), (), s32[]{:S(2)}) async-start(), calls=%async_computation.27 | async-start | bytes 786432 | tf_op jit(solution)/shard_map/reduce_scatter | solution.py:108
  93.0 53.5 %reduce-scatter.44.cloned.1.call-start = ((), (), s32[]{:S(2)}) async-start(), calls=%async_computation.32 | async-start | bytes 786432 | tf_op jit(solution)/shard_map/reduce_scatter | solution.py:108
  101.5 118.8 %reduce-scatter.58.cloned.1.call-start = ((), (), s32[]{:S(2)}) async-start(), calls=%async_computation.42 | async-start | bytes 6291456 | tf_op jit(solution)/shard_map/reduce_scatter | solution.py:100
  122.2 98.1 %reduce-scatter.46.cloned.1.call-start = ((), (), s32[]{:S(2)}) async-start(), calls=%async_computation.33 | async-start | bytes 12582912 | tf_op jit(solution)/shard_map/reduce_scatter | solution.py:100
  180.4 46.4 %reduce-scatter.50.cloned.1.call-start = ((), (), s32[]{:S(2)}) async-start(), calls=%async_computation.36 | async-start | bytes 6291456 | tf_op jit(solution)/shard_map/reduce_scatter | solution.py:100
  199.2 37.4 %reduce-scatter.38.cloned.1.call-start = ((), (), s32[]{:S(2)}) async-start(), calls=%async_computation.28 | async-start | bytes 12582912 | tf_op jit(solution)/shard_map/reduce_scatter | solution.py:100
  226.7 42.6 %all-gather.11.cloned.1.call-start = ((), (), s32[]{:S(2)}) async-start(), calls=%async_computation.37 | async-start | bytes 6291456 | tf_op jit(solution)/shard_map/all_gather | solution.py:104
  243.1 39.6 %all-gather.9.cloned.1.call-start = ((), (), s32[]{:S(2)}) async-start(), calls=%async_computation.34 | async-start | bytes 3145728 | tf_op jit(solution)/shard_map/all_gather | solution.py:104
  243.8 57.3 %reduce-scatter.60.cloned.1.call-start = ((), (), s32[]{:S(2)}) async-start(), calls=%async_computation.44 | async-start | bytes 786432 | tf_op jit(solution)/shard_map/reduce_scatter | solution.py:108
  263.2 55.4 %reduce-scatter.52.cloned.1.call-start = ((), (), s32[]{:S(2)}) async-start(), calls=%async_computation.38 | async-start | bytes 786432 | tf_op jit(solution)/shard_map/reduce_scatter | solution.py:108
  279.5 56.3 %reduce-scatter.48.cloned.1.call-start = ((), (), s32[]{:S(2)}) async-start(), calls=%async_computation.35 | async-start | bytes 786432 | tf_op jit(solution)/shard_map/reduce_scatter | solution.py:108
  289.9 72.9 %reduce-scatter.54.cloned.1.call-start = ((), (), s32[]{:S(2)}) async-start(), calls=%async_computation.39 | async-start | bytes 1572864 | tf_op jit(solution)/shard_map/reduce_scatter | solution.py:100
  360.4 45.5 %all-gather.13.cloned.1.call-start = ((), (), s32[]{:S(2)}) async-start(), calls=%async_computation.40 | async-start | bytes 2359296 | tf_op jit(solution)/shard_map/all_gather | solution.py:104
  405.9 147.3 %reduce-scatter.56.cloned.1.call-start = ((), (), s32[]{:S(2)}) async-start(), calls=%async_computation.41 | async-start | bytes 786432 | tf_op jit(solution)/shard_map/reduce_scatter | solution.py:108
  411.3 142.0 %reduce-scatter.64.cloned.1.call-start = ((), (), s32[]{:S(2)}) async-start(), calls=%async_computation.47 | async-start | bytes 786432 | tf_op jit(solution)/shard_map/reduce_scatter | solution.py:108
  421.3 141.4 %reduce-scatter.40.cloned.1.call-start = ((), (), s32[]{:S(2)}) async-start(), calls=%async_computation.30 | async-start | bytes 786432 | tf_op jit(solution)/shard_map/reduce_scatter | solution.py:108
  436.6 164.9 %reduce-scatter.66.cloned.1.call-start = ((), (), s32[]{:S(2)}) async-start(), calls=%async_computation.48 | async-start | bytes 2359296 | tf_op jit(solution)/shard_map/reduce_scatter | solution.py:286
  440.0 195.3 %reduce-scatter.74.cloned.1.call-start = ((), (), s32[]{:S(2)}) async-start(), calls=%async_computation.52 | async-start | bytes 2359296
  453.0 253.2 %reduce-scatter.72.cloned.1.call-start = ((), (), s32[]{:S(2)}) async-start(), calls=%async_computation.51 | async-start | bytes 2359296
  457.0 320.0 %reduce-scatter.70.cloned.1.call-start = ((), (), s32[]{:S(2)}) async-start(), calls=%async_computation.50 | async-start | bytes 2359296
  459.6 468.8 %reduce-scatter.68.cloned.1.call-start = ((), (), s32[]{:S(2)}) async-start(), calls=%async_computation.49 | async-start | bytes 9437184 | tf_op jit(solution)/shard_map/reduce_scatter | solution.py:298
  482.2 598.4 %reduce-scatter.78.cloned.1.call-start = ((), (), s32[]{:S(2)}) async-start(), calls=%async_computation.54 | async-start | bytes 9437184
  541.2 691.1 %reduce-scatter.76.cloned.1.call-start = ((), (), s32[]{:S(2)}) async-start(), calls=%async_computation.53 | async-start | bytes 9437184
  (94 other events, 827.0 us)
Sparse Core Ops, SparseCore 0:
  93.2 17.1 reduce-scatter.35
  113.1 14.2 reduce-scatter.43
  129.5 12.0 reduce-scatter.57
  180.6 16.6 reduce-scatter.45
  199.5 13.2 reduce-scatter.49
  219.9 16.6 reduce-scatter.37
  238.1 14.9 all-gather.14
  254.5 14.8 all-gather.10
  270.9 11.7 all-gather.8
  285.4 15.7 reduce-scatter.59
  304.0 14.5 reduce-scatter.51
  321.3 14.5 reduce-scatter.47
  405.2 10.7 all-gather.16
  417.6 11.7 all-gather.6
  432.2 15.7 reduce-scatter.55
  450.7 14.5 reduce-scatter.63
  468.2 14.5 reduce-scatter.39
  486.4 67.7 reduce-scatter.65
  557.6 77.6 reduce-scatter.73
  639.4 66.6 reduce-scatter.71
  710.1 66.8 reduce-scatter.69
  780.5 147.9 reduce-scatter.67
  932.5 148.0 reduce-scatter.77
  1084.2 147.9 reduce-scatter.75
  (5 shorter events, 47.9 us)
